TPU v7x, 32 devices: a whole 2x2x4 slice. The times are simulated.
32 devices in a mesh: groups: 2 (over y), space: 8 (over z, core), tm: 2 (over x), rep: 1.
Axes of the slice: x: 2, y: 2, z: 4, core: 2. Of those that a mesh axis runs over, the one named last changes fastest.
Arguments:
- noise: float32 [8192, 4096], P(('groups', 'space'), 'tm'), parts along dimension 0, may hold values from -6 to 6
- factor: float32 [4096, 4096], P(('tm', 'rep'), 'space'), may hold values from -8 to 8, as said below
- col_blocks: int32 [64, 4], P(('groups', 'space')), parts along dimension 0, may hold values from 0 to 31, as said below
- block_values: float32 [64, 4, 128, 128], P(('groups', 'space')), parts along dimension 0, may hold values from -0.25 to 0.25
Outputs:
- samples: float32 [8192, 4096], P(('groups', 'space'), ('tm', 'rep')), parts along dimension 0
There are 2 independent parts, one for each index of `groups`. A program takes and returns all parts, laid end to end along the dimension named above; an argument that names none is the same for every part. Nothing has to cross between parts.
Inputs may be any that keep to these rules, and one draw needn't show every extreme that they name: factor is lower triangular: every entry above the diagonal is zero, and the diagonal lies in 0.5 to 1.5. `col_blocks`: in every row b the first entry is b itself; the other 3 entries are distinct blocks whose circular distance from b (modulo 32) is 1 to 2.
All inputs are finite; a program needn't handle non-finite values.
Results may differ from a plain program's by a relative error of at most 0.0003.
Values sent between devices are 32-bit elements; how exact they have to be, the bound alone decides.
No kernel may reach another device: no remote copies, remote signals or barrier semaphores. Data moves between devices by JAX's collectives and lax.ppermute only.
A program may use at most 128 MiB of HBM per device.

v0:
```python
import jax
import jax.numpy as jnp
from jax import lax
from jax.sharding import PartitionSpec as P

BS = 128
REACH = 2


def shifted(block, axis, distance):
    devices = range(lax.axis_size(axis))
    route = [(i - distance, i) for i in devices if i - distance in devices]
    return lax.ppermute(block, axis, route)


def extended_2(block, sides, width):
    for axis, dim in sides:
        count = lax.axis_size(axis)
        forward = [(i, i + 1) for i in range(count - 1)]
        forward.append((count - 1, 0))
        backward = [(target, source) for source, target in forward]
        low = lax.ppermute(
            lax.slice_in_dim(block, block.shape[dim] - width, None, axis=dim), axis, forward
        )
        high = lax.ppermute(lax.slice_in_dim(block, 0, width, axis=dim), axis, backward)
        block = jnp.concatenate([low, block, high], axis=dim)
    return block


def per_device(noise, factor, col_blocks, block_values):
    node_rows = noise.shape[0]
    hour_cols = noise.shape[1]
    tm_index = lax.axis_index("tm")
    tm_count = lax.axis_size("tm")
    every_hour = jnp.zeros((node_rows, hour_cols * tm_count), jnp.float32)
    every_hour = lax.dynamic_update_slice_in_dim(every_hour, noise, tm_index * hour_cols, 1)
    moving = noise
    for step in range(1, tm_count):
        moving = shifted(moving, "tm", 1)
        slot = jnp.maximum(tm_index - step, 0) * hour_cols
        placed = lax.dynamic_update_slice_in_dim(every_hour, moving, slot, 1)
        every_hour = jnp.where(tm_index >= step, placed, every_hour)
    colored = lax.dot_general(
        every_hour,
        lax.all_gather(factor, "space", axis=1, tiled=True),
        (((1,), (1,)), ((), ())),
        precision=lax.Precision.HIGHEST,
        preferred_element_type=jnp.float32,
    )
    extended = extended_2(colored, (("space", 0),), REACH * BS)
    local_blocks = node_rows // BS
    out_cols = colored.shape[1]
    ext_blocks = extended.reshape(local_blocks + 2 * REACH, BS, out_cols)
    all_blocks = lax.axis_size("space") * local_blocks
    local_rows = jnp.arange(local_blocks, dtype=jnp.int32)[:, None]
    global_rows = lax.axis_index("space") * local_blocks + local_rows
    offsets = (col_blocks - global_rows + REACH) % all_blocks - REACH
    positions = local_rows + REACH + offsets
    picked = ext_blocks[positions]
    result = jnp.einsum("nkab,nkbh->nah", block_values, picked, precision=lax.Precision.HIGHEST)
    return result.reshape(node_rows, out_cols)


def solution(mesh):
    return jax.shard_map(
        per_device,
        mesh=mesh,
        in_specs=(
            P(("groups", "space"), "tm"),
            P(("tm", "rep"), "space"),
            P(("groups", "space"), None),
            P(("groups", "space"), None, None, None),
        ),
        out_specs=P(("groups", "space"), ("tm", "rep")),
        check_vma=False,
    )
```

profile of v0, /device:TPU:27, one launch (start us, length us, event | category | flops | bytes accessed | tf_op | source)
XLA Modules:
  0.0 446.1 jit_solution(9895273938419054406)
XLA Ops:
  6.5 0.0 copy-start
  6.5 0.0 all-gather.2.cloned.1.call-start
  6.5 0.7 all-gather.2.cloned.1.call-update
  7.3 1.3 collective-permute-start
  8.6 0.0 copy-start.2
  8.6 4.2 broadcast_in_dim.7
  12.8 0.0 copy-done.2
  12.8 2.2 constant_dynamic-update-slice_fusion
  15.1 85.9 %collective-permute-done = f32[512,2048]{1,0:T(8,128)} collective-permute-done((f32[512,2048]{1,0:T(8,128)}, f32[512,2048]{1,0:T(8,128)}, u32[]{:S(2)}, u32[]{:S(2)}) %collective-permute-start) | collective-permute-done | bytes 4194336 | tf_op jit(solution)/shard_map/ppermute | solution.py:13
  100.9 6.7 %select_dynamic-update-slice_fusion = f32[512,4096]{1,0:T(8,128)} fusion(f32[512,4096]{1,0:T(8,128)} %constant_dynamic-update-slice_fusion, s32[]{:T(128)S(6)} %select_n.30, f32[512,2048]{1,0:T(8,128)} %collective-permute-done, pred[]{:T(512)S(6)} %ge.3), kind=kLoop, calls=%fused_computation.2 | loop fusion | flops 1048576 | bytes 12582917 | tf_op jit(solution)/shard_map/jit(_where)/select_n | solution.py:42
  107.6 188.5 %all-gather.2.cloned.1.call-done = f32[2048,4096]{1,0:T(8,128)} async-done(((f32[2048,512]{1,0:T(8,128)}), f32[2048,4096]{1,0:T(8,128)}) %all-gather.2.cloned.1.call-update) | async-done | bytes 33554448 | tf_op jit(solution)/shard_map/all_gather | solution.py:45
  296.1 59.7 %fusion.4 = f32[512,2048]{1,0:T(8,128)S(1)} fusion(f32[512,4096]{1,0:T(8,128)} %select_dynamic-update-slice_fusion, f32[2048,4096]{1,0:T(8,128)} %all-gather.2.cloned.1.call-done), kind=kOutput, calls=%fused_computation.15 | convolution fusion | flops 51539607552 | bytes 46137344 | tf_op jit(solution)/shard_map/dot_general | solution.py:43
  355.8 0.0 copy-start.1
  355.9 2.0 copy-done.1
  357.9 0.0 copy-start.3
  357.9 1.6 fusion.3
  359.5 3.2 collective-permute-start.1
  362.7 0.0 collective-permute-start.2
  362.7 0.0 copy-done.3
  362.7 0.1 compare_select_fusion
  362.7 0.1 reshape.20
  362.8 44.4 %collective-permute-done.1 = f32[256,2048]{1,0:T(8,128)} collective-permute-done((f32[256,2048]{1,0:T(8,128)}, f32[256,2048]{1,0:T(8,128)}, u32[]{:S(2)}, u32[]{:S(2)}) %collective-permute-start.1) | collective-permute-done | bytes 2097184 | tf_op jit(solution)/shard_map/ppermute | solution.py:22
  407.2 1.5 collective-permute-done.2
  408.7 6.0 %pad_maximum_fusion = f32[1024,2048]{1,0:T(8,128)} fusion(f32[256,2048]{1,0:T(8,128)} %collective-permute-done.2, f32[512,2048]{1,0:T(8,128)} %copy-done.1, f32[256,2048]{1,0:T(8,128)} %collective-permute-done.1), kind=kLoop, calls=%fused_computation.1 | loop fusion | flops 4194304 | bytes 16777216 | tf_op jit(solution)/shard_map/concatenate | solution.py:26
  414.7 11.5 %gather_fusion = f32[16,128,2048]{2,1,0:T(8,128)} fusion(f32[8,128,2048]{2,1,0:T(8,128)} %bitcast.12, s32[1024]{0:T(1024)S(1)} %pad_clamp_fusion), kind=kCustom, calls=%fused_computation | custom fusion | bytes 33554496 | tf_op jit(solution)/shard_map/gather | solution.py:59
  426.2 0.0 copy-done
  426.2 13.1 %fusion.5 = f32[4,2048,128,1]{1,2,3,0:T(8,128)} fusion(f32[4,4,128,2048]{3,2,1,0:T(8,128)} %bitcast.13, f32[4,4,128,128]{3,2,1,0:T(8,128)S(1)} %copy-done), kind=kOutput, calls=%fused_computation.16 | convolution fusion | flops 6442450944 | bytes 22020096 | tf_op jit(solution)/shard_map/nkab,nkbh->nah/dot_general | solution.py:60
  (2 shorter events, 0.0 us)
Async XLA Ops:
  6.5 419.6 %copy-start = (f32[4,4,128,128]{3,2,1,0:T(8,128)S(1)}, f32[4,4,128,128]{3,2,1,0:T(8,128)}, u32[]{:S(2)}) copy-start(f32[4,4,128,128]{3,2,1,0:T(8,128)} %param.7) | copy-start | bytes 3145732
  6.5 289.6 %all-gather.2.cloned.1.call-start = ((), (), s32[]{:S(2)}) async-start(), calls=%async_computation | async-start | bytes 37748736 | tf_op jit(solution)/shard_map/all_gather | solution.py:45
  7.3 93.7 %collective-permute-start = (f32[512,2048]{1,0:T(8,128)}, f32[512,2048]{1,0:T(8,128)}, u32[]{:S(2)}, u32[]{:S(2)}) collective-permute-start(f32[512,2048]{1,0:T(8,128)} %param.4), channel_id=1, source_target_pairs={{0,1},{2,3},{4,5},{6,7},{8,9},{10,11},{12,13},{14,15},{16,17},{18,... | collective-permute-start | bytes 12582920 | tf_op jit(solution)/shard_map/ppermute | solution.py:13
  8.6 4.3 copy-start.2
  355.8 2.0 copy-start.1
  357.9 4.8 %copy-start.3 = (s32[4,4]{1,0:T(4,128)S(1)}, s32[4,4]{1,0:T(4,128)}, u32[]{:S(2)}) copy-start(s32[4,4]{1,0:T(4,128)} %param.6) | copy-start | bytes 196
  359.5 47.8 %collective-permute-start.1 = (f32[256,2048]{1,0:T(8,128)}, f32[256,2048]{1,0:T(8,128)}, u32[]{:S(2)}, u32[]{:S(2)}) collective-permute-start(f32[256,2048]{1,0:T(8,128)} %get-tuple-element.5), channel_id=1, source_target_pairs={{0,2},{2,4},{4,6},{6,8},{8,10},{10,12},{12,14},{14,0},{1,3},{3,5},... | collective-permute-start | bytes 6291464 | tf_op jit(solution)/shard_map/ppermute | solution.py:22
  362.7 46.1 %collective-permute-start.2 = (f32[256,2048]{1,0:T(8,128)S(1)}, f32[256,2048]{1,0:T(8,128)}, u32[]{:S(2)}, u32[]{:S(2)}) collective-permute-start(f32[256,2048]{1,0:T(8,128)S(1)} %get-tuple-element.6), channel_id=1, source_target_pairs={{2,0},{4,2},{6,4},{8,6},{10,8},{12,10},{14,12},{0,14},{3,1},{5,3},... | collective-permute-start | bytes 6291464 | tf_op jit(solution)/shard_map/ppermute | solution.py:25
Sparse Core Ops, SparseCore 0:
  8.9 287.1 all-gather.1
where the time goes:
time: 450 us; the launch traced here: 446 us
  waiting for transfers between devices  321 us (71%)
  matrix products  72.8 us (16%)
  local copies, waits for them, and re-layouts  21.7 us (5%)
  between operations  13.4 us (3%)
  other arithmetic  12.8 us (3%)
    all_gather x1, waiting for transfers between devices, per_device(): lax.all_gather(factor, 'space', axis=1, tiled=True)  188 us
    ppermute x1, waiting for transfers between devices, shifted(): return lax.ppermute(block, axis, route)  85.9 us
    dot_general x1, matrix products, per_device(): lax.dot_general(every_hour, lax.all_gather(factor, 'space', axis=1, tiled...  59.7 us
    ppermute x1, waiting for transfers between devices, extended_2(): lax.ppermute(lax.slice_in_dim(block, block.shape[dim] - width, None, axis...  44.4 us
    dot_general x1, matrix products, per_device(): jnp.einsum('nkab,nkbh->nah', block_values, picked, precision=lax.Precisio...  13.1 us
    gather x1, local copies, waits for them, and re-layouts, per_device(): picked = ext_blocks[positions]  11.5 us
  transfers between devices with their start and end apart: 4, of which 4 were waited for; matrix products, arithmetic and copies ran while one was open for 3% of the time, Pallas kernels for 0%

commit v1 on v0

--- a/solution.py
+++ b/solution.py
@@ -1,10 +1,21 @@
+import functools
+
 import jax
 import jax.numpy as jnp
 from jax import lax
+from jax.experimental import pallas as pl
+from jax.experimental.pallas import tpu as pltpu
 from jax.sharding import PartitionSpec as P
 
 BS = 128
 REACH = 2
+F32 = jnp.float32
+BF16 = jnp.bfloat16
+ANY = pl.BlockSpec(memory_space=pl.ANY)
+VMEM = pl.BlockSpec(memory_space=pltpu.VMEM)
+SMEM = pl.BlockSpec(memory_space=pltpu.SMEM)
+NT = (((1,), (1,)), ((), ()))
+NN = (((1,), (0,)), ((), ()))
 
 
 def shifted(block, axis, distance):
@@ -27,12 +38,12 @@
     return block
 
 
-def per_device(noise, factor, col_blocks, block_values):
+def general(noise, factor, col_blocks, block_values):
     node_rows = noise.shape[0]
     hour_cols = noise.shape[1]
     tm_index = lax.axis_index("tm")
     tm_count = lax.axis_size("tm")
-    every_hour = jnp.zeros((node_rows, hour_cols * tm_count), jnp.float32)
+    every_hour = jnp.zeros((node_rows, hour_cols * tm_count), F32)
     every_hour = lax.dynamic_update_slice_in_dim(every_hour, noise, tm_index * hour_cols, 1)
     moving = noise
     for step in range(1, tm_count):
@@ -45,7 +56,7 @@
         lax.all_gather(factor, "space", axis=1, tiled=True),
         (((1,), (1,)), ((), ())),
         precision=lax.Precision.HIGHEST,
-        preferred_element_type=jnp.float32,
+        preferred_element_type=F32,
     )
     extended = extended_2(colored, (("space", 0),), REACH * BS)
     local_blocks = node_rows // BS
@@ -61,9 +72,337 @@
     return result.reshape(node_rows, out_cols)
 
 
+def split(value):
+    high = value.astype(BF16)
+    return high, (value - high.astype(F32)).astype(BF16)
+
+
+def precision_kernel(side, scal, cols, values, own_keep, own_send, far_keep, far_send, keep, send, hi, lo):
+    core, first, total = scal[3], scal[5], scal[6]
+    half = far_keep.shape[0]
+    for own, far, out in ((own_keep, far_keep, keep), (own_send, far_send, send)):
+        own_at = 0 if side == "mid" else half
+        far_at = 2 * half if side == "mid" else 0
+        for part in range(2):
+            at = own_at + jnp.where(core == 0, part, 1 - part) * half
+            at = pl.multiple_of(at, half)
+            high, low = split(own[part * half : (part + 1) * half, :])
+            hi[pl.ds(at, half), :] = high
+            lo[pl.ds(at, half), :] = low
+        high, low = split(far[...])
+        hi[far_at : far_at + half, :] = high
+        lo[far_at : far_at + half, :] = low
+        rows = half // BS
+        for i in range(rows):
+            mid_rows = core == 0 if side == "mid" else core == 1
+            row = i + jnp.where(mid_rows, rows, 0)
+            picked_hi, picked_lo, left = [], [], []
+            for k in range(values.shape[1]):
+                offset = cols[row, k] - first - row
+                offset = lax.rem(offset + REACH + 2 * total, total) - REACH
+                place = row + REACH + offset
+                group = place // REACH
+                group = jnp.where(core == 0, group, 3 - group)
+                group = group - (1 if side == "mid" else 0)
+                group = jnp.clip(group, 0, 2)
+                at = pl.multiple_of((group * REACH + lax.rem(place, REACH)) * BS, BS)
+                picked_hi.append(hi[pl.ds(at, BS), :])
+                picked_lo.append(lo[pl.ds(at, BS), :])
+                left.append(values[i, k])
+            left_hi, left_lo = split(jnp.concatenate(left, axis=1))
+            right_hi = jnp.concatenate(picked_hi, axis=0)
+            right_lo = jnp.concatenate(picked_lo, axis=0)
+            acc = lax.dot_general(left_hi, right_hi, NN, preferred_element_type=F32)
+            acc += lax.dot_general(left_lo, right_hi, NN, preferred_element_type=F32)
+            acc += lax.dot_general(left_hi, right_lo, NN, preferred_element_type=F32)
+            out[i * BS : (i + 1) * BS, :] = acc
+
+
+def precision(side, scal, cols, values, own, far, tile):
+    half, hours = far.shape
+    nodes = own.shape[0]
+    pairs = hours // (2 * tile)
+    kept = lambda q, s, c: (0, 2 * q + s[3])
+    sent = lambda q, s, c: (0, 2 * q + 1 - s[3])
+    at = (lambda q, s, c: (1 - s[3], 0, 0, 0)) if side == "mid" else (lambda q, s, c: (s[3], 0, 0, 0))
+    piece = jax.ShapeDtypeStruct((half, hours // 2), F32)
+    return pl.pallas_call(
+        functools.partial(precision_kernel, side),
+        out_shape=(piece, piece),
+        grid_spec=pltpu.PrefetchScalarGridSpec(
+            num_scalar_prefetch=2,
+            grid=(pairs,),
+            in_specs=[
+                pl.BlockSpec((half // BS,) + values.shape[1:], at),
+                pl.BlockSpec((nodes, tile), kept),
+                pl.BlockSpec((nodes, tile), sent),
+                pl.BlockSpec((half, tile), kept),
+                pl.BlockSpec((half, tile), sent),
+            ],
+            out_specs=[pl.BlockSpec((half, tile), lambda q, s, c: (0, q))] * 2,
+            scratch_shapes=[pltpu.VMEM((3 * half, tile), BF16)] * 2,
+        ),
+        compiler_params=pltpu.CompilerParams(vmem_limit_bytes=24 << 20),
+        cost_estimate=pl.CostEstimate(
+            flops=6 * half * values.shape[1] * BS * hours, bytes_accessed=16 * half * hours, transcendentals=0
+        ),
+        name="precision_" + side,
+    )(scal, cols, values, own, own, far, far)
+
+
+def prepare_kernel(scal, mine, theirs, *refs):
+    tile = mine.shape[1]
+    for piece, out in ((mine, refs[-2]), (theirs, refs[-1])):
+        high, low = split(piece[...])
+        out[0, :, :tile] = high
+        out[0, :, tile:] = low
+
+
+def prepare(scal, mine, theirs, outer, received, before, tile):
+    half, width = mine.shape
+    tiles = width // tile
+
+    def place(q, s):
+        owner = 1 - s[1] if received else s[1]
+        return (owner * tiles + q, outer, 0)
+
+    whole = jax.ShapeDtypeStruct((2 * tiles, 2 * half, 2 * tile), BF16)
+    return pl.pallas_call(
+        prepare_kernel,
+        out_shape=(whole, whole),
+        grid_spec=pltpu.PrefetchScalarGridSpec(
+            num_scalar_prefetch=1,
+            grid=(tiles,),
+            in_specs=[pl.BlockSpec((half, tile), lambda q, s: (0, q))] * 2 + [ANY] * len(before),
+            out_specs=[pl.BlockSpec((1, half, 2 * tile), place)] * 2,
+        ),
+        input_output_aliases={3: 0, 4: 1} if before else {},
+        compiler_params=pltpu.CompilerParams(vmem_limit_bytes=16 << 20),
+        cost_estimate=pl.CostEstimate(flops=0, bytes_accessed=16 * half * width, transcendentals=0),
+        name="prepare",
+    )(scal, mine, theirs, *before)
+
+
+def multiply_kernel(jobs, band, first, scal, mine, theirs, *refs):
+    refs = list(refs)
+    before = [] if first else [refs.pop(0), refs.pop(0)]
+    count = 1 + max(source for source, _, _, _ in jobs)
+    sources = [refs.pop(0) for _ in range(count)]
+    acc_mine, acc_theirs, buf, both, low, sems = refs
+    group, hour, chip, core = scal[0], scal[1], scal[2], scal[3]
+    chips = scal[4]
+    height, width = buf.shape[1:]
+    nrows = acc_mine.shape[1]
+    step = min(256, nrows)
+
+    plan = []
+    for n, (source, row, hop, kind) in enumerate(jobs):
+        owner = chip + hop
+        where = row if kind == "own" else group if kind == "direct" else 1 - group
+        bottom = hour * (4 * height) + (2 * band + where + 1) * height
+        valid = (owner >= 0) & (owner < chips) & ((2 * owner + core) * width < bottom)
+        src = sources[source]
+        if kind == "own":
+            src = src.at[pl.ds((2 * band + row) * height, height), :]
+        plan.append((valid, owner, where, pltpu.make_async_copy(src, buf.at[n], sems.at[n])))
+    for valid, _, _, copy in plan:
+        pl.when(valid)(copy.start)
+
+    for r in range(acc_mine.shape[0]):
+        for out, old in zip((acc_mine, acc_theirs), before or (None, None)):
+            @pl.loop(0, nrows // step)
+            def _(m):
+                at = pl.ds(pl.multiple_of(m * step, step), step)
+                out[r, at, :] = jnp.zeros((step, height), F32) if first else old[r, at, :]
+
+    for n, (valid, owner, where, copy) in enumerate(plan):
+        @pl.when(valid)
+        def _():
+            copy.wait()
+
+            @pl.loop(0, height // 128)
+            def _(m):
+                at = pl.ds(pl.multiple_of(m * 128, 128), 128)
+                hi, lo = split(buf[n, at, :])
+                both[at, :width] = hi
+                both[at, width:] = hi
+                low[at, :] = lo
+
+            for out, left in ((acc_theirs, theirs), (acc_mine, mine)):
+                @pl.loop(0, nrows // step)
+                def _(m):
+                    at = pl.ds(pl.multiple_of(m * step, step), step)
+                    acc = lax.dot_general(left[owner, at, :], both[...], NT, preferred_element_type=F32)
+                    acc += lax.dot_general(left[owner, at, :width], low[...], NT, preferred_element_type=F32)
+                    out[where, at, :] += acc
+
+
+def multiply(jobs, sources, band, scal, ready, before, height, width):
+    nrows = ready[0].shape[1]
+    piece = jax.ShapeDtypeStruct((2, nrows, height), F32)
+    inputs = (scal,) + tuple(ready) + tuple(before) + tuple(sources)
+    return pl.pallas_call(
+        functools.partial(multiply_kernel, jobs, band, not before),
+        out_shape=(piece, piece),
+        in_specs=[SMEM] + [VMEM] * (2 + len(before)) + [ANY] * len(sources),
+        out_specs=[VMEM, VMEM],
+        scratch_shapes=[
+            pltpu.VMEM((len(jobs), height, width), F32),
+            pltpu.VMEM((height, 2 * width), BF16),
+            pltpu.VMEM((height, width), BF16),
+            pltpu.SemaphoreType.DMA((len(jobs),)),
+        ],
+        input_output_aliases={3: 0, 4: 1} if before else {},
+        compiler_params=pltpu.CompilerParams(vmem_limit_bytes=36 << 20),
+        cost_estimate=pl.CostEstimate(
+            flops=12 * nrows * height * width * max(1, len(jobs) // 2), bytes_accessed=16 << 20, transcendentals=0
+        ),
+        name="multiply_%d_%d" % (band, len(jobs)),
+    )(*inputs)
+
+
+def finish_kernel(scal, left, right, *refs):
+    refs[-1][...] = left[0] + right[0]
+
+
+def finish(scal, band, mine, received, before, hours):
+    pieces, nrows, height = mine.shape
+    half = nrows // 2
+    from_acc = pl.BlockSpec((1, half, height), lambda i, r, s: (r, i, 0))
+
+    def place(i, r, s):
+        return (jnp.where(s[3] == 0, 1 - i, i), pieces * band + r)
+
+    return pl.pallas_call(
+        finish_kernel,
+        out_shape=jax.ShapeDtypeStruct((nrows, hours), F32),
+        grid_spec=pltpu.PrefetchScalarGridSpec(
+            num_scalar_prefetch=1,
+            grid=(2, pieces),
+            in_specs=[from_acc, from_acc] + [ANY] * len(before),
+            out_specs=pl.BlockSpec((half, height), place),
+        ),
+        input_output_aliases={3: 0} if before else {},
+        compiler_params=pltpu.CompilerParams(vmem_limit_bytes=16 << 20),
+        cost_estimate=pl.CostEstimate(
+            flops=nrows * height * pieces, bytes_accessed=12 * nrows * height * pieces, transcendentals=0
+        ),
+        name="finish_%d" % band,
+    )(scal, mine, received, *before)
+
+
+def paired(noise, factor, col_blocks, block_values):
+    node_rows, hours = noise.shape
+    height, width = factor.shape[0] // 4, factor.shape[1]
+    half = node_rows // 2
+    space = lax.axis_size("space")
+    chips = space // 2
+    tm = lax.axis_size("tm")
+    group, place, hour = lax.axis_index("groups"), lax.axis_index("space"), lax.axis_index("tm")
+    chip, core = place // 2, place % 2
+    blocks = node_rows // BS
+    scal = jnp.stack([group, hour, chip, core, jnp.int32(chips), place * blocks, jnp.int32(space * blocks)])
+
+    other_core = [(i, i ^ 1) for i in range(space)]
+    across = [(i, (i + 1) % space) for i in range(1, space, 2)]
+    across += [(target, source) for source, target in across]
+
+    def device(z, c, x):
+        return (2 * z + c) * tm + x
+
+    def carried(band, x, z):
+        return 2 * z * width < (4 * x + 2 * band + 2) * height
+
+    def along(chunk, band, hop):
+        sign = 1 if hop < 0 else -1
+        route = []
+        for z in range(chips):
+            begin = z + hop + sign
+            if 0 <= begin < chips and 0 <= z + sign < chips:
+                route += [
+                    (device(z, c, x), device(z + sign, c, x)) for c in range(2) for x in range(tm) if carried(band, x, begin)
+                ]
+        return lax.ppermute(chunk, ("space", "tm"), route) if route else None
+
+    def swapped(chunk, band, hop):
+        count = space * tm
+        route = []
+        for z in range(chips):
+            if 0 <= z + hop < chips:
+                for c in range(2):
+                    for x in range(tm):
+                        if carried(band, x, z + hop):
+                            d = device(z, c, x)
+                            route += [(d, count + d), (count + d, d)]
+        return lax.ppermute(chunk, ("groups", "space", "tm"), route)
+
+    mid = lax.dynamic_slice_in_dim(noise, half * (1 - core), half, 0)
+    outer = lax.dynamic_slice_in_dim(noise, half * core, half, 0)
+    far_mid = lax.ppermute(mid, "space", other_core)
+    far_outer = lax.ppermute(outer, "space", across)
+
+    received = {}
+    moving = {}
+    for band in (1, 0):
+        chunk = lax.dynamic_slice_in_dim(factor, (2 * band + group) * height, height, 0)
+        moving[band, 1], moving[band, -1] = chunk, chunk
+    for distance in range(1, chips):
+        for band in (1, 0):
+            for sign in (1, -1):
+                hop = -sign * distance
+                chunk = along(moving[band, sign], band, hop)
+                if chunk is not None:
+                    moving[band, sign] = chunk
+                    received[band, hop] = [chunk, swapped(chunk, band, hop)]
+
+    ready = ()
+    pieces = {}
+    for outside, (side, far) in enumerate((("mid", far_mid), ("outer", far_outer))):
+        keep, send = precision(side, scal, col_blocks, block_values, noise, far, width)
+        theirs = lax.ppermute(send, "space", other_core)
+        pieces[outside] = (keep, theirs)
+        ready = prepare(scal, keep, theirs, outside, False, ready, width)
+    for outside in range(2):
+        later = [lax.ppermute(piece, "tm", [(0, 1)]) for piece in pieces[outside]]
+        ready = prepare(scal, later[0], later[1], outside, True, ready, width)
+
+    sums = {0: (), 1: ()}
+    for distance in range(1, chips):
+        for band in (1, 0):
+            jobs, sources = [], []
+            if distance == 1:
+                sources.append(factor)
+                jobs += [(0, 0, 0, "own"), (0, 1, 0, "own")]
+            for hop in (-distance, distance):
+                if (band, hop) in received:
+                    for chunk, kind in zip(received[band, hop], ("direct", "swapped")):
+                        jobs.append((len(sources), 0, hop, kind))
+                        sources.append(chunk)
+            sums[band] = multiply(jobs, sources, band, scal, ready, sums[band], height, width)
+    out = ()
+    for band in (1, 0):
+        mine, theirs = sums[band]
+        out = (finish(scal, band, mine, lax.ppermute(theirs, "space", other_core), out, 4 * height),)
+    return out[0]
+
+
+def fits(mesh):
+    shape = mesh.shape
+    return shape["groups"] == 2 and shape["tm"] == 2 and shape["rep"] == 1 and shape["space"] % 2 == 0 and shape["space"] >= 4
+
+
+def per_device(mesh, noise, factor, col_blocks, block_values):
+    rows, width = factor.shape
+    nodes, hours = noise.shape
+    square = fits(mesh) and nodes == 4 * BS and rows == 4 * width and hours == rows and rows * 2 == width * mesh.shape["space"]
+    if square and width % 128 == 0 and REACH * BS * 2 == nodes:
+        return paired(noise, factor, col_blocks, block_values)
+    return general(noise, factor, col_blocks, block_values)
+
+
 def solution(mesh):
     return jax.shard_map(
-        per_device,
+        functools.partial(per_device, mesh),
         mesh=mesh,
         in_specs=(
             P(("groups", "space"), "tm"),

time: 450 us -> 318 us (0.71)
  waiting for transfers between devices: 321 us -> 184 us
  matrix products: 72.8 us -> 0 us
  Pallas kernels: 0 us -> 59.7 us
  starting transfers between devices: 4.49 us -> 62.4 us
  between operations: 13.4 us -> 0.48 us
  other arithmetic: 12.8 us -> 0 us
  local copies, waits for them, and re-layouts: 21.7 us -> 10.3 us
    all_gather x1 -> x0, waiting for transfers between devices: 188 us -> none  [per_device(): lax.all_gather(factor, 'space', axis=1, tiled=True)]
    dot_general x2 -> x0, matrix products: 72.8 us -> none  [the longest x1 59.7 us: per_device(): lax.dot_general(every_hour, lax.all_gather(factor, 'space', axis=1, tiled...]
    pallas_call x0 -> x14, Pallas kernels: none -> 59.7 us  [the longest x6 41.4 us: multiply(): pl.pallas_call(functools.partial(multiply_kernel, jobs, band, not before)...]
    ppermute x3 -> x32, starting transfers between devices: 4.49 us -> 62.4 us  [the longest x11 19.3 us: swapped(): return lax.ppermute(chunk, ('groups', 'space', 'tm'), route)]
    ppermute x3 -> x32, waiting for transfers between devices: 132 us -> 184 us  [the longest x11 85.5 us: along(): return lax.ppermute(chunk, ('space', 'tm'), route) if route else None]
    gather x1 -> x0, local copies, waits for them, and re-layouts: 11.5 us -> none  [per_device(): picked = ext_blocks[positions]]
    select_n x2 -> x0, other arithmetic: 6.79 us -> none  [the longest x1 6.71 us: per_device(): every_hour = jnp.where(tm_index >= step, placed, every_hour)]
    concatenate x1 -> x0, other arithmetic: 5.98 us -> none  [extended_2(): block = jnp.concatenate([low, block, high], axis=dim)]
  transfers between devices with their start and end apart: 4 -> 32, of which waited for: 4 -> 12; matrix products, arithmetic and copies ran while one was open for 3% -> 1% of each run, Pallas kernels for 0% -> 18%
where the time goes in v1:
time: 318 us; the launch traced here: 317 us
  waiting for transfers between devices  184 us (58%)
  starting transfers between devices  62.4 us (20%)
  Pallas kernels  59.7 us (19%)
  local copies, waits for them, and re-layouts  10.3 us (3%)
    ppermute x11, waiting for transfers between devices, along(): return lax.ppermute(chunk, ('space', 'tm'), route) if route else None  85.5 us
    ppermute x4, waiting for transfers between devices, paired(): later = [lax.ppermute(piece, 'tm', [(0, 1)]) for piece in pieces[outside]]  71.9 us
    pallas_call x6, Pallas kernels, multiply(): pl.pallas_call(functools.partial(multiply_kernel, jobs, band, not before)...  41.4 us
    ppermute x11, waiting for transfers between devices, swapped(): return lax.ppermute(chunk, ('groups', 'space', 'tm'), route)  25.3 us
    ppermute x11, starting transfers between devices, swapped(): return lax.ppermute(chunk, ('groups', 'space', 'tm'), route)  19.3 us
    ppermute x11, starting transfers between devices, along(): return lax.ppermute(chunk, ('space', 'tm'), route) if route else None  15.6 us
    ppermute x2, starting transfers between devices, paired(): theirs = lax.ppermute(send, 'space', other_core)  12.4 us
    pallas_call x2, Pallas kernels, precision(): pl.pallas_call(functools.partial(precision_kernel, side), out_shape=(piec...  9 us
  transfers between devices with their start and end apart: 32, of which 12 were waited for; matrix products, arithmetic and copies ran while one was open for 1% of the time, Pallas kernels for 18%

profile of v1, /device:TPU:27, one launch (start us, length us, event | category | flops | bytes accessed | tf_op | source)
XLA Modules:
  0.0 317.0 jit_solution(3187132166446122490)
XLA Ops:
  0.0 3.0 constant_dynamic-slice_fusion
  4.4 2.6 constant_dynamic-slice_fusion.2
  7.8 3.0 collective-permute-start
  10.8 2.3 collective-permute-start.21
  13.1 1.6 collective-permute-start.10
  14.7 14.6 %collective-permute-done.19.refs_1_ = f32[512,512]{1,0:T(8,128)} collective-permute-done((f32[512,512]{1,0:T(8,128)}, f32[512,512]{1,0:T(8,128)}, u32[]{:S(2)}, u32[]{:S(2)}) %collective-permute-start.19) | collective-permute-done | bytes 1048608 | tf_op jit(solution)/shard_map/ppermute | solution.py:325
  29.3 1.3 collective-permute-start.8
  30.6 48.2 %collective-permute-done.21.refs_3_ = f32[512,512]{1,0:T(8,128)} collective-permute-done((f32[512,512]{1,0:T(8,128)}, f32[512,512]{1,0:T(8,128)}, u32[]{:S(2)}, u32[]{:S(2)}) %collective-permute-start.21) | collective-permute-done | bytes 1048608 | tf_op jit(solution)/shard_map/ppermute | solution.py:325
  78.8 3.1 collective-permute-start.20
  81.9 1.6 collective-permute-start.22
  83.6 14.2 %collective-permute-done.8.refs_1_ = f32[512,512]{1,0:T(8,128)} collective-permute-done((f32[512,512]{1,0:T(8,128)S(1)}, f32[512,512]{1,0:T(8,128)}, u32[]{:S(2)}, u32[]{:S(2)}) %collective-permute-start.8) | collective-permute-done | bytes 1048608 | tf_op jit(solution)/shard_map/ppermute | solution.py:325
  97.7 1.3 collective-permute-start.23
  99.0 1.6 collective-permute-start.25
  100.7 1.3 copy-done.1
  103.3 2.0 collective-permute-done.20.refs_2_
  106.2 1.6 collective-permute-start.14
  108.0 2.2 copy-done
  110.1 4.5 %precision_mid.1 = (f32[256,1024]{1,0:T(8,128)S(1)}, f32[256,1024]{1,0:T(8,128)S(1)}) custom-call(s32[7]{0:T(128)S(1)} %stack.23.scal, s32[4,4]{1,0:T(4,128)S(1)} %copy-done.4, f32[4,4,128,128]{3,2,1,0:T(8,128)S(1)} %copy-done.3, f32[512,2048]{1,0:T(8,128)S(1)} %copy-done, f32[512,2048]{1,0:T(8,128)S(1)} %copy-done, ...), custom_call_target="tpu_custom_call" | custom-call | flops 1610612736 | bytes 8388608 | tf_op jit(solution)/shard_map/precision_mid/pallas_call | solution.py:129
  114.6 4.5 %precision_outer.1 = (f32[256,1024]{1,0:T(8,128)S(1)}, f32[256,1024]{1,0:T(8,128)S(1)}) custom-call(s32[7]{0:T(128)S(1)} %stack.23.scal, s32[4,4]{1,0:T(4,128)S(1)} %copy-done.4, f32[4,4,128,128]{3,2,1,0:T(8,128)S(1)} %copy-done.3, f32[512,2048]{1,0:T(8,128)S(1)} %copy-done, f32[512,2048]{1,0:T(8,128)S(1)} %copy-done, f32[256,2048]{1,0:T(8,128)S(1)} %copy-done.2, ...), custom_call_target="tpu_custom_call" | custom-call | flops 1610612736 | bytes 8388608 | tf_op jit(solution)/shard_map/precision_outer/pallas_call | solution.py:129
  120.4 11.2 %collective-permute-start.2 = (f32[256,1024]{1,0:T(8,128)S(1)}, f32[256,1024]{1,0:T(8,128)S(1)}, u32[]{:S(2)}, u32[]{:S(2)}) collective-permute-start(f32[256,1024]{1,0:T(8,128)S(1)} %get-tuple-element.30), channel_id=1, source_target_pairs={{0,2},{2,0},{4,6},{6,4},{8,10},{10,8},{12,14},{14,12},{1,3},{3,1},... | collective-permute-start | bytes 3145736 | tf_op jit(solution)/shard_map/ppermute | solution.py:362
  131.6 1.3 collective-permute-start.5
  132.9 8.6 %collective-permute-done.12.refs_2_ = f32[512,512]{1,0:T(8,128)} collective-permute-done((f32[512,512]{1,0:T(8,128)}, f32[512,512]{1,0:T(8,128)}, u32[]{:S(2)}, u32[]{:S(2)}) %collective-permute-start.12) | collective-permute-done | bytes 1048608 | tf_op jit(solution)/shard_map/ppermute | solution.py:325
  141.5 1.3 collective-permute-start.1
  142.8 1.3 collective-permute-start.27
  144.8 1.3 collective-permute-start.7
  146.1 12.1 %collective-permute-done.5.mine = f32[256,1024]{1,0:T(8,128)S(1)} collective-permute-done((f32[256,1024]{1,0:T(8,128)S(1)}, f32[256,1024]{1,0:T(8,128)S(1)}, u32[]{:S(2)}, u32[]{:S(2)}) %collective-permute-start.5) | collective-permute-done | bytes 1048608 | tf_op jit(solution)/shard_map/ppermute | solution.py:366
  159.5 21.2 %collective-permute-done.1.mine = f32[256,1024]{1,0:T(8,128)S(1)} collective-permute-done((f32[256,1024]{1,0:T(8,128)S(1)}, f32[256,1024]{1,0:T(8,128)S(1)}, u32[]{:S(2)}, u32[]{:S(2)}) %collective-permute-start.1) | collective-permute-done | bytes 1048608 | tf_op jit(solution)/shard_map/ppermute | solution.py:366
  180.7 2.1 collective-permute-start.24
  183.6 1.3 collective-permute-start.16
  184.9 18.3 %collective-permute-done.7.theirs = f32[256,1024]{1,0:T(8,128)S(1)} collective-permute-done((f32[256,1024]{1,0:T(8,128)S(1)}, f32[256,1024]{1,0:T(8,128)S(1)}, u32[]{:S(2)}, u32[]{:S(2)}) %collective-permute-start.7) | collective-permute-done | bytes 1048608 | tf_op jit(solution)/shard_map/ppermute | solution.py:366
  203.2 2.1 collective-permute-start.28
  205.3 20.3 %collective-permute-done.3.theirs = f32[256,1024]{1,0:T(8,128)S(1)} collective-permute-done((f32[256,1024]{1,0:T(8,128)S(1)}, f32[256,1024]{1,0:T(8,128)S(1)}, u32[]{:S(2)}, u32[]{:S(2)}) %collective-permute-start.3) | collective-permute-done | bytes 1048608 | tf_op jit(solution)/shard_map/ppermute | solution.py:366
  231.6 2.1 collective-permute-start.9
  233.8 9.9 %multiply_1_6.1 = (f32[2,512,512]{2,1,0:T(8,128)S(1)}, f32[2,512,512]{2,1,0:T(8,128)S(1)}) custom-call(s32[7]{0:T(128)S(1)} %stack.23.scal, bf16[4,512,1024]{2,1,0:T(8,128)(2,1)S(1)} %get-tuple-element.39.mine, bf16[4,512,1024]{2,1,0:T(8,128)(2,1)S(1)} %get-tuple-element.40.theirs, f32[2048,512]{1,0:T(8,128)} %refs_0_.3, ...), custom_call_target="tpu_custom_call" | custom-call | flops 4831838208 | bytes 16777216 | tf_op jit(solution)/shard_map/multiply_1_6/pallas_call | solution.py:244
  243.6 3.2 collective-permute-start.13
  247.6 7.0 %multiply_1_4.2 = (f32[2,512,512]{2,1,0:T(8,128)S(1)}, f32[2,512,512]{2,1,0:T(8,128)S(1)}) custom-call(s32[7]{0:T(128)S(1)} %stack.23.scal, bf16[4,512,1024]{2,1,0:T(8,128)(2,1)S(1)} %get-tuple-element.39.mine, bf16[4,512,1024]{2,1,0:T(8,128)(2,1)S(1)} %get-tuple-element.40.theirs, ...), custom_call_target="tpu_custom_call", output_to_operand_aliasing={{0}: (3, {}), {1}: (4, {})} | custom-call | flops 3221225472 | bytes 16777216 | tf_op jit(solution)/shard_map/multiply_1_4/pallas_call | solution.py:244
  254.6 2.1 collective-permute-start.17
  256.8 6.5 %multiply_1_4.3 = (f32[2,512,512]{2,1,0:T(8,128)S(1)}, f32[2,512,512]{2,1,0:T(8,128)S(1)}) custom-call(s32[7]{0:T(128)S(1)} %stack.23.scal, bf16[4,512,1024]{2,1,0:T(8,128)(2,1)S(1)} %get-tuple-element.39.mine, bf16[4,512,1024]{2,1,0:T(8,128)(2,1)S(1)} %get-tuple-element.40.theirs, ...), custom_call_target="tpu_custom_call", output_to_operand_aliasing={{0}: (3, {}), {1}: (4, {})} | custom-call | flops 3221225472 | bytes 16777216 | tf_op jit(solution)/shard_map/multiply_1_4/pallas_call | solution.py:244
  263.3 4.4 %collective-permute-start.31 = (f32[2,512,512]{2,1,0:T(8,128)S(1)}, f32[2,512,512]{2,1,0:T(8,128)S(1)}, u32[]{:S(2)}, u32[]{:S(2)}) collective-permute-start(f32[2,512,512]{2,1,0:T(8,128)S(1)} %get-tuple-element.52), channel_id=1, source_target_pairs={{0,2},{2,0},{4,6},{6,4},{8,10},{10,8},{12,14},{14,12},{1,3},{3,1},... | collective-permute-start | bytes 6291464 | tf_op jit(solution)/shard_map/ppermute | solution.py:385
  267.7 4.5 %multiply_0_6.1 = (f32[2,512,512]{2,1,0:T(8,128)S(1)}, f32[2,512,512]{2,1,0:T(8,128)S(1)}) custom-call(s32[7]{0:T(128)S(1)} %stack.23.scal, bf16[4,512,1024]{2,1,0:T(8,128)(2,1)S(1)} %get-tuple-element.39.mine, bf16[4,512,1024]{2,1,0:T(8,128)(2,1)S(1)} %get-tuple-element.40.theirs, f32[2048,512]{1,0:T(8,128)} %refs_0_.3, ...), custom_call_target="tpu_custom_call" | custom-call | flops 4831838208 | bytes 16777216 | tf_op jit(solution)/shard_map/multiply_0_6/pallas_call | solution.py:244
  272.1 7.9 %collective-permute-done.13.refs_3_ = f32[512,512]{1,0:T(8,128)S(1)} collective-permute-done((f32[512,512]{1,0:T(8,128)}, f32[512,512]{1,0:T(8,128)S(1)}, u32[]{:S(2)}, u32[]{:S(2)}) %collective-permute-start.13) | collective-permute-done | bytes 1048608 | tf_op jit(solution)/shard_map/ppermute | solution.py:337
  280.1 7.0 %multiply_0_4.1 = (f32[2,512,512]{2,1,0:T(8,128)S(1)}, f32[2,512,512]{2,1,0:T(8,128)S(1)}) custom-call(s32[7]{0:T(128)S(1)} %stack.23.scal, bf16[4,512,1024]{2,1,0:T(8,128)(2,1)S(1)} %get-tuple-element.39.mine, bf16[4,512,1024]{2,1,0:T(8,128)(2,1)S(1)} %get-tuple-element.40.theirs, ...), custom_call_target="tpu_custom_call", output_to_operand_aliasing={{0}: (3, {}), {1}: (4, {})} | custom-call | flops 3221225472 | bytes 16777216 | tf_op jit(solution)/shard_map/multiply_0_4/pallas_call | solution.py:244
  287.1 15.4 %collective-permute-done.17.refs_3_ = f32[512,512]{1,0:T(8,128)S(1)} collective-permute-done((f32[512,512]{1,0:T(8,128)S(1)}, f32[512,512]{1,0:T(8,128)S(1)}, u32[]{:S(2)}, u32[]{:S(2)}) %collective-permute-start.17) | collective-permute-done | bytes 1048608 | tf_op jit(solution)/shard_map/ppermute | solution.py:337
  302.5 6.5 %multiply_0_2.1 = (f32[2,512,512]{2,1,0:T(8,128)S(1)}, f32[2,512,512]{2,1,0:T(8,128)S(1)}) custom-call(s32[7]{0:T(128)S(1)} %stack.23.scal, bf16[4,512,1024]{2,1,0:T(8,128)(2,1)S(1)} %get-tuple-element.39.mine, bf16[4,512,1024]{2,1,0:T(8,128)(2,1)S(1)} %get-tuple-element.40.theirs, ...), custom_call_target="tpu_custom_call", output_to_operand_aliasing={{0}: (3, {}), {1}: (4, {})} | custom-call | flops 1610612736 | bytes 16777216 | tf_op jit(solution)/shard_map/multiply_0_2/pallas_call | solution.py:244
  309.0 1.8 collective-permute-start.18
  310.8 2.4 finish_1.1.refs_0_
  313.2 1.3 collective-permute-done.18.right
  314.6 2.4 finish_0.1
  (49 shorter events, 15.0 us)
Async XLA Ops:
  3.0 26.2 %collective-permute-start.19 = (f32[512,512]{1,0:T(8,128)}, f32[512,512]{1,0:T(8,128)}, u32[]{:S(2)}, u32[]{:S(2)}) collective-permute-start(f32[512,512]{1,0:T(8,128)} %get-tuple-element.53), channel_id=1, source_target_pairs={{0,4},{1,5},{2,6},{3,7},{4,8},{5,9},{6,10},{7,11},{9,13},{11,15},{... | collective-permute-start | bytes 3145736 | tf_op jit(solution)/shard_map/ppermute | solution.py:325
  4.4 8.7 %copy-start.7 = (f32[512,512]{1,0:T(8,128)S(1)}, f32[512,512]{1,0:T(8,128)}, u32[]{:S(2)}) copy-start(f32[512,512]{1,0:T(8,128)} %get-tuple-element.54) | copy-start | bytes 3145732
  4.4 103.6 %copy-start.3 = (f32[4,4,128,128]{3,2,1,0:T(8,128)S(1)}, f32[4,4,128,128]{3,2,1,0:T(8,128)}, u32[]{:S(2)}) copy-start(f32[4,4,128,128]{3,2,1,0:T(8,128)} %values.3) | copy-start | bytes 3145732
  4.4 103.6 %copy-start.4 = (s32[4,4]{1,0:T(4,128)S(1)}, s32[4,4]{1,0:T(4,128)}, u32[]{:S(2)}) copy-start(s32[4,4]{1,0:T(4,128)} %cols.3) | copy-start | bytes 196
  7.0 92.0 %collective-permute-start.4 = (f32[256,2048]{1,0:T(8,128)S(1)}, f32[256,2048]{1,0:T(8,128)S(1)}, u32[]{:S(2)}, u32[]{:S(2)}) collective-permute-start(f32[256,2048]{1,0:T(8,128)S(1)} %get-tuple-element.55), channel_id=1, source_target_pairs={{0,2},{2,0},{4,6},{6,4},{8,10},{10,8},{12,14},{14,12},{1,3},{3,1},... | collective-permute-start | bytes 6291464 | tf_op jit(solution)/shard_map/ppermute | solution.py:341
  7.8 92.9 %collective-permute-start = (f32[256,2048]{1,0:T(8,128)S(1)}, f32[256,2048]{1,0:T(8,128)S(1)}, u32[]{:S(2)}, u32[]{:S(2)}) collective-permute-start(f32[256,2048]{1,0:T(8,128)S(1)} %get-tuple-element.56), channel_id=1, source_target_pairs={{2,4},{6,8},{10,12},{14,0},{4,2},{8,6},{12,10},{0,14},{3,5},{7,9},... | collective-permute-start | bytes 6291464 | tf_op jit(solution)/shard_map/ppermute | solution.py:342
  10.8 68.0 %collective-permute-start.21 = (f32[512,512]{1,0:T(8,128)}, f32[512,512]{1,0:T(8,128)}, u32[]{:S(2)}, u32[]{:S(2)}) collective-permute-start(f32[512,512]{1,0:T(8,128)} %get-tuple-element.53), channel_id=1, source_target_pairs={{4,0},{5,1},{6,2},{7,3},{9,5},{11,7},{13,9},{15,11},{20,16},{21,17... | collective-permute-start | bytes 3145736 | tf_op jit(solution)/shard_map/ppermute | solution.py:325
  13.1 68.8 %collective-permute-start.10 = (f32[512,512]{1,0:T(8,128)S(1)}, f32[512,512]{1,0:T(8,128)}, u32[]{:S(2)}, u32[]{:S(2)}) collective-permute-start(f32[512,512]{1,0:T(8,128)S(1)} %copy-done.7), channel_id=1, source_target_pairs={{5,1},{7,3},{9,5},{11,7},{21,17},{23,19},{25,21},{27,23}} | collective-permute-start | bytes 3145736 | tf_op jit(solution)/shard_map/ppermute | solution.py:325
  29.3 68.4 %collective-permute-start.8 = (f32[512,512]{1,0:T(8,128)S(1)}, f32[512,512]{1,0:T(8,128)}, u32[]{:S(2)}, u32[]{:S(2)}) collective-permute-start(f32[512,512]{1,0:T(8,128)S(1)} %copy-done.7), channel_id=1, source_target_pairs={{0,4},{1,5},{2,6},{3,7},{5,9},{7,11},{9,13},{11,15},{16,20},{17,21... | collective-permute-start | bytes 3145736 | tf_op jit(solution)/shard_map/ppermute | solution.py:325
  78.8 26.5 %collective-permute-start.20 = (f32[512,512]{1,0:T(8,128)}, f32[512,512]{1,0:T(8,128)S(1)}, u32[]{:S(2)}, u32[]{:S(2)}) collective-permute-start(f32[512,512]{1,0:T(8,128)} %collective-permute-done.19.refs_1_), channel_id=1, source_target_pairs={{4,20},{20,4},{5,21},{21,5},{6,22},{22,6},{7,23},{23,7},{8,24},{24... | collective-permute-start | bytes 3145736 | tf_op jit(solution)/shard_map/ppermute | solution.py:337
  81.9 37.3 %collective-permute-start.22 = (f32[512,512]{1,0:T(8,128)}, f32[512,512]{1,0:T(8,128)}, u32[]{:S(2)}, u32[]{:S(2)}) collective-permute-start(f32[512,512]{1,0:T(8,128)} %collective-permute-done.21.refs_3_), channel_id=1, source_target_pairs={{0,16},{16,0},{1,17},{17,1},{2,18},{18,2},{3,19},{19,3},{5,21},{21... | collective-permute-start | bytes 3145736 | tf_op jit(solution)/shard_map/ppermute | solution.py:337
  97.7 22.7 %collective-permute-start.23 = (f32[512,512]{1,0:T(8,128)}, f32[512,512]{1,0:T(8,128)}, u32[]{:S(2)}, u32[]{:S(2)}) collective-permute-start(f32[512,512]{1,0:T(8,128)} %collective-permute-done.19.refs_1_), channel_id=1, source_target_pairs={{4,8},{5,9},{6,10},{7,11},{8,12},{9,13},{10,14},{11,15},{20,24},{2... | collective-permute-start | bytes 3145736 | tf_op jit(solution)/shard_map/ppermute | solution.py:325
  99.0 32.6 %collective-permute-start.25 = (f32[512,512]{1,0:T(8,128)}, f32[512,512]{1,0:T(8,128)}, u32[]{:S(2)}, u32[]{:S(2)}) collective-permute-start(f32[512,512]{1,0:T(8,128)} %collective-permute-done.21.refs_3_), channel_id=1, source_target_pairs={{5,1},{7,3},{9,5},{11,7},{21,17},{23,19},{25,21},{27,23}} | collective-permute-start | bytes 3145736 | tf_op jit(solution)/shard_map/ppermute | solution.py:325
  100.7 1.3 copy-start.1
  102.0 39.5 %collective-permute-start.12 = (f32[512,512]{1,0:T(8,128)}, f32[512,512]{1,0:T(8,128)}, u32[]{:S(2)}, u32[]{:S(2)}) collective-permute-start(f32[512,512]{1,0:T(8,128)} %collective-permute-done.8.refs_1_), channel_id=1, source_target_pairs={{4,8},{5,9},{6,10},{7,11},{9,13},{11,15},{20,24},{21,25},{22,26},{... | collective-permute-start | bytes 3145736 | tf_op jit(solution)/shard_map/ppermute | solution.py:325
  105.3 1.0 copy-start.5
  106.2 36.5 %collective-permute-start.14 = (f32[512,512]{1,0:T(8,128)}, f32[512,512]{1,0:T(8,128)}, u32[]{:S(2)}, u32[]{:S(2)}) collective-permute-start(f32[512,512]{1,0:T(8,128)} %collective-permute-done.10.refs_3_), channel_id=1, source_target_pairs={{5,1},{7,3},{21,17},{23,19}} | collective-permute-start | bytes 3145736 | tf_op jit(solution)/shard_map/ppermute | solution.py:325
  108.0 2.2 copy-start
  110.1 4.5 %copy-start.2 = (f32[256,2048]{1,0:T(8,128)S(1)}, f32[256,2048]{1,0:T(8,128)}, u32[]{:S(2)}) copy-start(f32[256,2048]{1,0:T(8,128)} %copy-done.1) | copy-start | bytes 6291460
  119.2 24.9 %collective-permute-start.6 = (f32[256,1024]{1,0:T(8,128)S(1)}, f32[256,1024]{1,0:T(8,128)S(1)}, u32[]{:S(2)}, u32[]{:S(2)}) collective-permute-start(f32[256,1024]{1,0:T(8,128)S(1)} %get-tuple-element.32), channel_id=1, source_target_pairs={{0,2},{2,0},{4,6},{6,4},{8,10},{10,8},{12,14},{14,12},{1,3},{3,1},... | collective-permute-start | bytes 3145736 | tf_op jit(solution)/shard_map/ppermute | solution.py:362
  120.4 24.4 %collective-permute-start.2 = (f32[256,1024]{1,0:T(8,128)S(1)}, f32[256,1024]{1,0:T(8,128)S(1)}, u32[]{:S(2)}, u32[]{:S(2)}) collective-permute-start(f32[256,1024]{1,0:T(8,128)S(1)} %get-tuple-element.30), channel_id=1, source_target_pairs={{0,2},{2,0},{4,6},{6,4},{8,10},{10,8},{12,14},{14,12},{1,3},{3,1},... | collective-permute-start | bytes 3145736 | tf_op jit(solution)/shard_map/ppermute | solution.py:362
  131.6 26.6 %collective-permute-start.5 = (f32[256,1024]{1,0:T(8,128)S(1)}, f32[256,1024]{1,0:T(8,128)S(1)}, u32[]{:S(2)}, u32[]{:S(2)}) collective-permute-start(f32[256,1024]{1,0:T(8,128)S(1)} %get-tuple-element.31.mine), channel_id=1, source_target_pairs={{0,1},{2,3},{4,5},{6,7},{8,9},{10,11},{12,13},{14,15},{16,17},{18,... | collective-permute-start | bytes 3145736 | tf_op jit(solution)/shard_map/ppermute | solution.py:366
  141.5 39.2 %collective-permute-start.1 = (f32[256,1024]{1,0:T(8,128)S(1)}, f32[256,1024]{1,0:T(8,128)S(1)}, u32[]{:S(2)}, u32[]{:S(2)}) collective-permute-start(f32[256,1024]{1,0:T(8,128)S(1)} %get-tuple-element.29.mine), channel_id=1, source_target_pairs={{0,1},{2,3},{4,5},{6,7},{8,9},{10,11},{12,13},{14,15},{16,17},{18,... | collective-permute-start | bytes 3145736 | tf_op jit(solution)/shard_map/ppermute | solution.py:366
  142.8 40.1 %collective-permute-start.27 = (f32[512,512]{1,0:T(8,128)}, f32[512,512]{1,0:T(8,128)S(1)}, u32[]{:S(2)}, u32[]{:S(2)}) collective-permute-start(f32[512,512]{1,0:T(8,128)} %collective-permute-done.23.refs_2_), channel_id=1, source_target_pairs={{8,12},{9,13},{10,14},{11,15},{24,28},{25,29},{26,30},{27,31}} | collective-permute-start | bytes 3145736 | tf_op jit(solution)/shard_map/ppermute | solution.py:325
  144.1 39.5 %collective-permute-start.29 = (f32[512,512]{1,0:T(8,128)}, f32[512,512]{1,0:T(8,128)S(1)}, u32[]{:S(2)}, u32[]{:S(2)}) collective-permute-start(f32[512,512]{1,0:T(8,128)} %collective-permute-done.25.refs_4_), channel_id=1, source_target_pairs={{5,1},{7,3},{21,17},{23,19}} | collective-permute-start | bytes 3145736 | tf_op jit(solution)/shard_map/ppermute | solution.py:325
  144.8 58.3 %collective-permute-start.7 = (f32[256,1024]{1,0:T(8,128)S(1)}, f32[256,1024]{1,0:T(8,128)S(1)}, u32[]{:S(2)}, u32[]{:S(2)}) collective-permute-start(f32[256,1024]{1,0:T(8,128)S(1)} %collective-permute-done.6.theirs), channel_id=1, source_target_pairs={{0,1},{2,3},{4,5},{6,7},{8,9},{10,11},{12,13},{14,15},{16,17},{18,... | collective-permute-start | bytes 3145736 | tf_op jit(solution)/shard_map/ppermute | solution.py:366
  158.2 67.4 %collective-permute-start.3 = (f32[256,1024]{1,0:T(8,128)S(1)}, f32[256,1024]{1,0:T(8,128)S(1)}, u32[]{:S(2)}, u32[]{:S(2)}) collective-permute-start(f32[256,1024]{1,0:T(8,128)S(1)} %collective-permute-done.2.theirs), channel_id=1, source_target_pairs={{0,1},{2,3},{4,5},{6,7},{8,9},{10,11},{12,13},{14,15},{16,17},{18,... | collective-permute-start | bytes 3145736 | tf_op jit(solution)/shard_map/ppermute | solution.py:366
  180.7 50.2 %collective-permute-start.24 = (f32[512,512]{1,0:T(8,128)}, f32[512,512]{1,0:T(8,128)S(1)}, u32[]{:S(2)}, u32[]{:S(2)}) collective-permute-start(f32[512,512]{1,0:T(8,128)} %collective-permute-done.23.refs_2_), channel_id=1, source_target_pairs={{8,24},{24,8},{9,25},{25,9},{10,26},{26,10},{11,27},{27,11},{12,28... | collective-permute-start | bytes 3145736 | tf_op jit(solution)/shard_map/ppermute | solution.py:337
  182.8 48.8 %collective-permute-start.26 = (f32[512,512]{1,0:T(8,128)}, f32[512,512]{1,0:T(8,128)S(1)}, u32[]{:S(2)}, u32[]{:S(2)}) collective-permute-start(f32[512,512]{1,0:T(8,128)} %collective-permute-done.25.refs_4_), channel_id=1, source_target_pairs={{1,17},{17,1},{3,19},{19,3},{5,21},{21,5},{7,23},{23,7}} | collective-permute-start | bytes 3145736 | tf_op jit(solution)/shard_map/ppermute | solution.py:337
  183.6 60.1 %collective-permute-start.16 = (f32[512,512]{1,0:T(8,128)}, f32[512,512]{1,0:T(8,128)S(1)}, u32[]{:S(2)}, u32[]{:S(2)}) collective-permute-start(f32[512,512]{1,0:T(8,128)} %collective-permute-done.12.refs_2_), channel_id=1, source_target_pairs={{8,12},{9,13},{10,14},{11,15},{24,28},{25,29},{26,30},{27,31}} | collective-permute-start | bytes 3145736 | tf_op jit(solution)/shard_map/ppermute | solution.py:325
  203.2 43.7 %collective-permute-start.28 = (f32[512,512]{1,0:T(8,128)S(1)}, f32[512,512]{1,0:T(8,128)S(1)}, u32[]{:S(2)}, u32[]{:S(2)}) collective-permute-start(f32[512,512]{1,0:T(8,128)S(1)} %collective-permute-done.27.refs_2_), channel_id=1, source_target_pairs={{12,28},{28,12},{13,29},{29,13},{14,30},{30,14},{15,31},{31,15}} | collective-permute-start | bytes 3145736 | tf_op jit(solution)/shard_map/ppermute | solution.py:337
  225.6 29.0 %collective-permute-start.30 = (f32[512,512]{1,0:T(8,128)S(1)}, f32[512,512]{1,0:T(8,128)S(1)}, u32[]{:S(2)}, u32[]{:S(2)}) collective-permute-start(f32[512,512]{1,0:T(8,128)S(1)} %collective-permute-done.29.refs_4_), channel_id=1, source_target_pairs={{1,17},{17,1},{3,19},{19,3}} | collective-permute-start | bytes 3145736 | tf_op jit(solution)/shard_map/ppermute | solution.py:337
  229.7 4.0 %copy-start.6 = (f32[512,512]{1,0:T(8,128)S(1)}, f32[512,512]{1,0:T(8,128)}, u32[]{:S(2)}) copy-start(f32[512,512]{1,0:T(8,128)} %copy-done.5) | copy-start | bytes 3145732
  230.9 32.4 %collective-permute-start.11 = (f32[512,512]{1,0:T(8,128)}, f32[512,512]{1,0:T(8,128)S(1)}, u32[]{:S(2)}, u32[]{:S(2)}) collective-permute-start(f32[512,512]{1,0:T(8,128)} %collective-permute-done.10.refs_3_), channel_id=1, source_target_pairs={{1,17},{17,1},{3,19},{19,3},{5,21},{21,5},{7,23},{23,7}} | collective-permute-start | bytes 3145736 | tf_op jit(solution)/shard_map/ppermute | solution.py:337
  231.6 36.0 %collective-permute-start.9 = (f32[512,512]{1,0:T(8,128)}, f32[512,512]{1,0:T(8,128)}, u32[]{:S(2)}, u32[]{:S(2)}) collective-permute-start(f32[512,512]{1,0:T(8,128)} %collective-permute-done.8.refs_1_), channel_id=1, source_target_pairs={{4,20},{20,4},{5,21},{21,5},{6,22},{22,6},{7,23},{23,7},{9,25},{25... | collective-permute-start | bytes 3145736 | tf_op jit(solution)/shard_map/ppermute | solution.py:337
  243.6 36.4 %collective-permute-start.13 = (f32[512,512]{1,0:T(8,128)}, f32[512,512]{1,0:T(8,128)S(1)}, u32[]{:S(2)}, u32[]{:S(2)}) collective-permute-start(f32[512,512]{1,0:T(8,128)} %collective-permute-done.12.refs_2_), channel_id=1, source_target_pairs={{8,24},{24,8},{9,25},{25,9},{10,26},{26,10},{11,27},{27,11},{13,29... | collective-permute-start | bytes 3145736 | tf_op jit(solution)/shard_map/ppermute | solution.py:337
  246.8 33.2 %collective-permute-start.15 = (f32[512,512]{1,0:T(8,128)}, f32[512,512]{1,0:T(8,128)S(1)}, u32[]{:S(2)}, u32[]{:S(2)}) collective-permute-start(f32[512,512]{1,0:T(8,128)} %collective-permute-done.14.refs_4_), channel_id=1, source_target_pairs={{1,17},{17,1},{3,19},{19,3}} | collective-permute-start | bytes 3145736 | tf_op jit(solution)/shard_map/ppermute | solution.py:337
  254.6 47.9 %collective-permute-start.17 = (f32[512,512]{1,0:T(8,128)S(1)}, f32[512,512]{1,0:T(8,128)S(1)}, u32[]{:S(2)}, u32[]{:S(2)}) collective-permute-start(f32[512,512]{1,0:T(8,128)S(1)} %collective-permute-done.16.refs_2_), channel_id=1, source_target_pairs={{12,28},{28,12},{13,29},{29,13},{14,30},{30,14},{15,31},{31,15}} | collective-permute-start | bytes 3145736 | tf_op jit(solution)/shard_map/ppermute | solution.py:337
  263.3 47.5 %collective-permute-start.31 = (f32[2,512,512]{2,1,0:T(8,128)S(1)}, f32[2,512,512]{2,1,0:T(8,128)S(1)}, u32[]{:S(2)}, u32[]{:S(2)}) collective-permute-start(f32[2,512,512]{2,1,0:T(8,128)S(1)} %get-tuple-element.52), channel_id=1, source_target_pairs={{0,2},{2,0},{4,6},{6,4},{8,10},{10,8},{12,14},{14,12},{1,3},{3,1},... | collective-permute-start | bytes 6291464 | tf_op jit(solution)/shard_map/ppermute | solution.py:385
  309.0 5.6 %collective-permute-start.18 = (f32[2,512,512]{2,1,0:T(8,128)S(1)}, f32[2,512,512]{2,1,0:T(8,128)S(1)}, u32[]{:S(2)}, u32[]{:S(2)}) collective-permute-start(f32[2,512,512]{2,1,0:T(8,128)S(1)} %get-tuple-element.46), channel_id=1, source_target_pairs={{0,2},{2,0},{4,6},{6,4},{8,10},{10,8},{12,14},{14,12},{1,3},{3,1},... | collective-permute-start | bytes 6291464 | tf_op jit(solution)/shard_map/ppermute | solution.py:385
